TPU v7x, 512 devices: a whole 4x4x16 slice. The times are simulated.
512 devices in a mesh: cuts: 128 (over z, x, core), stem: 4 (over y).
Axes of the slice: x: 4, y: 4, z: 16, core: 2. Of those that a mesh axis runs over, the one named last changes fastest.
Arguments:
- stem_tensor: bfloat16 [8, 64, 1024], P('stem'), may hold values from -6 to 6
- mid_tensors: bfloat16 [8192, 512, 128], P(('cuts', 'stem')), may hold values from -0.1875 to 0.1875
- right_tensors: bfloat16 [8, 8192, 64, 128], P(None, ('cuts', 'stem')), may hold values from -0.001953125 to 0.001953125
Outputs:
- amplitudes: float32 [8192], P('cuts')
All inputs are finite; a program needn't handle non-finite values.
Results may differ from a plain program's by a relative error of at most 0.0029.
Values may be sent and summed in bfloat16 or wider, within the bound.
A program may use at most 64 MiB of HBM per device.

v0:
```python
import jax
import jax.numpy as jnp
from jax import lax
from jax.sharding import PartitionSpec as P


def widen(tensor):
    half_width = tensor.shape[-1] // 2
    real_part = tensor[..., :half_width]
    imag_part = tensor[..., half_width:]
    upper_rows = jnp.concatenate([real_part, imag_part], axis=-1)
    lower_rows = jnp.concatenate([-imag_part, real_part], axis=-1)
    return jnp.concatenate([upper_rows, lower_rows], axis=-2)


def on_device(stem_tensor, mid_tensors, right_tensors):
    local_blocks, rows_a, width = stem_tensor.shape
    cols_b = right_tensors.shape[-1]
    widened = jnp.moveaxis(widen(mid_tensors), 0, 1).reshape(width, -1)
    fragment = lax.all_gather(stem_tensor, "stem", axis=0, tiled=True)
    flattened = fragment.reshape(-1, width)
    product = jnp.dot(flattened, widened, preferred_element_type=jnp.float32)
    first_step = product.astype(jnp.bfloat16).reshape(fragment.shape[0], rows_a, -1)
    right_wide = widen(right_tensors).reshape(first_step.shape[0], -1, cols_b)
    partial_sum = jnp.einsum(
        "iaq,iqb->ab", first_step, right_wide, preferred_element_type=jnp.float32
    ).reshape(-1)
    summed = lax.psum(partial_sum, ("cuts", "stem"))
    portion = partial_sum.shape[0] // lax.axis_size("cuts")
    return lax.dynamic_slice_in_dim(summed, lax.axis_index("cuts") * portion, portion)


def solution(mesh):
    return jax.shard_map(
        on_device,
        mesh=mesh,
        in_specs=(
            P("stem", None, None),
            P(("cuts", "stem"), None, None),
            P(None, ("cuts", "stem"), None, None),
        ),
        out_specs=P("cuts"),
        check_vma=False,
    )
```

profile of v0, /device:TPU:1, one launch (start us, length us, event | category | flops | bytes accessed | tf_op | source)
XLA Modules:
  0.0 163.8 jit_solution(10493150595197969950)
XLA Ops:
  6.5 0.0 all-gather.2.cloned.1.call-start
  6.5 0.7 all-gather.2.cloned.1.call-update
  7.3 2.9 %copy.9 = bf16[16,512,128]{1,2,0:T(8,128)(2,1)S(1)} copy(bf16[16,512,128]{2,1,0:T(8,128)(2,1)} %param.4) | data formatting | bytes 4194304 | tf_op args[1]
  10.1 0.1 slice_negate_fusion.1
  10.3 0.0 copy-start.1
  10.3 2.2 %maximum_maximum_fusion = bf16[16,1024,128]{1,2,0:T(8,128)(2,1)} fusion(bf16[16,512,64]{1,2,0:T(8,128)(2,1)S(1)} %get-tuple-element.8, bf16[16,512,64]{1,2,0:T(8,128)(2,1)S(1)} %get-tuple-element.7, bf16[16,512,128]{1,2,0:T(8,128)(2,1)S(1)} %copy.9), kind=kLoop, calls=%fused_computation | loop fusion | flops 12582912 | bytes 8388608 | tf_op jit(solution)/shard_map/concatenate | solution.py:13
  12.5 0.1 copy-done.1
  12.6 0.9 slice_negate_fusion
  13.5 3.5 %maximum_maximum_fusion.1 = bf16[8,16,128,128]{3,2,1,0:T(8,128)(2,1)} fusion(bf16[8,16,64,64]{3,2,1,0:T(8,128)(2,1)S(1)} %get-tuple-element.6, bf16[8,16,64,64]{3,2,1,0:T(8,128)(2,1)S(1)} %get-tuple-element.5, bf16[8,16,64,128]{3,2,1,0:T(8,128)(2,1)S(1)} %copy-done.1), kind=kLoop, calls=%fused_computation.1 | loop fusion | flops 12582912 | bytes 8388608 | tf_op jit(solution)/shard_map/concatenate | solution.py:13
  17.0 28.6 %all-gather.2.cloned.1.call-done = bf16[8,64,1024]{2,1,0:T(8,128)(2,1)} async-done(((bf16[2,64,1024]{2,1,0:T(8,128)(2,1)}), bf16[8,64,1024]{2,1,0:T(8,128)(2,1)}) %all-gather.2.cloned.1.call-update) | async-done | bytes 1048592 | tf_op jit(solution)/shard_map/all_gather | solution.py:20
  45.6 0.0 copy-start
  45.6 5.0 %convolution_convert_fusion = bf16[2048,512]{0,1:T(8,128)(2,1)S(1)} fusion(bf16[1024,2048]{0,1:T(8,128)(2,1)} %bitcast.18, bf16[512,1024]{1,0:T(8,128)(2,1)} %bitcast.19), kind=kOutput, calls=%fused_computation.2 | convolution fusion | flops 2148532224 | bytes 7340032 | tf_op jit(solution)/shard_map/dot_general | solution.py:22
  50.6 0.0 copy-done
  50.6 0.9 convolution_bitcast_fusion
  51.4 105.0 %psum.7 = f32[8192]{0:T(1024)S(1)} all-reduce(f32[8192]{0:T(1024)S(1)} %convolution_bitcast_fusion), channel_id=1, replica_groups=mesh['cuts'=128,'stem'=4] {'cuts','stem'}, use_global_device_ids=true, to_apply=%region_0.0 | all-reduce | flops 8192 | bytes 65536 | tf_op jit(solution)/shard_map/psum | solution.py:28
  156.4 0.6 dynamic_slice.3
Async XLA Ops:
  6.5 39.0 %all-gather.2.cloned.1.call-start = ((), (), s32[]{:S(2)}) async-start(), calls=%async_computation | async-start | bytes 1310720 | tf_op jit(solution)/shard_map/all_gather | solution.py:20
  10.3 2.3 %copy-start.1 = (bf16[8,16,64,128]{3,2,1,0:T(8,128)(2,1)S(1)}, bf16[8,16,64,128]{3,2,1,0:T(8,128)(2,1)}, u32[]{:S(2)}) copy-start(bf16[8,16,64,128]{3,2,1,0:T(8,128)(2,1)} %param.5) | copy-start | bytes 6291460
  45.6 5.0 %copy-start = (bf16[8,16,128,128]{3,2,1,0:T(8,128)(2,1)S(1)}, bf16[8,16,128,128]{3,2,1,0:T(8,128)(2,1)}, u32[]{:S(2)}) copy-start(bf16[8,16,128,128]{3,2,1,0:T(8,128)(2,1)} %maximum_maximum_fusion.1) | copy-start | bytes 12582916
Sparse Core Ops, SparseCore 0:
  9.5 36.0 all-gather.1
where the time goes:
time: 164 us
  blocking collectives  105 us (64%)
  waiting for transfers between devices  29.3 us (18%)
  between operations  13.4 us (8%)
  other arithmetic  6.78 us (4%)
  matrix products  5.86 us (4%)
  local copies, waits for them, and re-layouts  3.52 us (2%)
    psum x1, blocking collectives, on_device(): summed = lax.psum(partial_sum, ('cuts', 'stem'))  105 us
    all_gather x1, waiting for transfers between devices, on_device(): fragment = lax.all_gather(stem_tensor, 'stem', axis=0, tiled=True)  28.6 us
    concatenate x2, other arithmetic, widen(): return jnp.concatenate([upper_rows, lower_rows], axis=-2)  5.77 us
    dot_general x1, matrix products, on_device(): product = jnp.dot(flattened, widened, preferred_element_type=jnp.float32)  5.01 us
  transfers between devices with their start and end apart: 1, of which 1 were waited for; matrix products, arithmetic and copies ran while one was open for 6% of the time, Pallas kernels for 0%

commit v1 on v0

--- a/solution.py
+++ b/solution.py
@@ -17,7 +17,26 @@
     local_blocks, rows_a, width = stem_tensor.shape
     cols_b = right_tensors.shape[-1]
     widened = jnp.moveaxis(widen(mid_tensors), 0, 1).reshape(width, -1)
-    fragment = lax.all_gather(stem_tensor, "stem", axis=0, tiled=True)
+    size, index, width_2 = (lax.axis_size("stem"), lax.axis_index("stem"), stem_tensor.shape[0])
+    right = [(i, (i + 1) % size) for i in range(size)]
+    left = [(i, (i - 1) % size) for i in range(size)]
+    result = jnp.zeros(
+        (*stem_tensor.shape[:0], size * width_2, *stem_tensor.shape[0 + 1 :]), stem_tensor.dtype
+    )
+    result = lax.dynamic_update_slice_in_dim(result, stem_tensor, index * width_2, axis=0)
+    from_left = from_right = stem_tensor
+    halfway = size // 2
+    for step in range(1, halfway + 1):
+        from_left = lax.ppermute(from_left, "stem", right)
+        result = lax.dynamic_update_slice_in_dim(
+            result, from_left, (index - step) % size * width_2, axis=0
+        )
+        if step < size - halfway:
+            from_right = lax.ppermute(from_right, "stem", left)
+            result = lax.dynamic_update_slice_in_dim(
+                result, from_right, (index + step) % size * width_2, axis=0
+            )
+    fragment = result
     flattened = fragment.reshape(-1, width)
     product = jnp.dot(flattened, widened, preferred_element_type=jnp.float32)
     first_step = product.astype(jnp.bfloat16).reshape(fragment.shape[0], rows_a, -1)

time: 164 us -> 146 us (0.89)
  waiting for transfers between devices: 29.3 us -> 6.1 us
  between operations: 13.4 us -> 0.2 us
  starting transfers between devices: 0.01 us -> 9.43 us
  blocking collectives: 105 us -> 111 us
  local copies, waits for them, and re-layouts: 3.52 us -> 5.44 us
    all_gather x1 -> x0, waiting for transfers between devices: 28.6 us -> none  [on_device(): fragment = lax.all_gather(stem_tensor, 'stem', axis=0, tiled=True)]
    ppermute x0 -> x3, starting transfers between devices: none -> 9.43 us  [the longest x1 5.59 us: on_device(): from_right = lax.ppermute(from_right, 'stem', left)]
    ppermute x0 -> x3, waiting for transfers between devices: none -> 6.1 us  [the longest x2 6.09 us: on_device(): from_left = lax.ppermute(from_left, 'stem', right)]
    psum x1, blocking collectives: 105 us -> 111 us  [on_device(): summed = lax.psum(partial_sum, ('cuts', 'stem'))]
    unnamed x5 -> x9, local copies, waits for them, and re-layouts: 2.94 us -> 4.65 us
  transfers between devices with their start and end apart: 1 -> 3, of which waited for: 1 -> 1; matrix products, arithmetic and copies ran while one was open for 6% -> 9% of each run, Pallas kernels for 0% -> 0%
where the time goes in v1:
time: 146 us
  blocking collectives  111 us (76%)
  starting transfers between devices  9.43 us (6%)
  other arithmetic  8.32 us (6%)
  waiting for transfers between devices  6.1 us (4%)
  matrix products  5.56 us (4%)
  local copies, waits for them, and re-layouts  5.44 us (4%)
    psum x1, blocking collectives, on_device(): summed = lax.psum(partial_sum, ('cuts', 'stem'))  111 us
    ppermute x2, waiting for transfers between devices, on_device(): from_left = lax.ppermute(from_left, 'stem', right)  6.09 us
    concatenate x2, other arithmetic, widen(): return jnp.concatenate([upper_rows, lower_rows], axis=-2)  5.76 us
    ppermute x1, starting transfers between devices, on_device(): from_right = lax.ppermute(from_right, 'stem', left)  5.59 us
    dot_general x1, matrix products, on_device(): product = jnp.dot(flattened, widened, preferred_element_type=jnp.float32)  4.7 us
    unnamed x9, local copies, waits for them, and re-layouts  4.65 us
    ppermute x2, starting transfers between devices, on_device(): from_left = lax.ppermute(from_left, 'stem', right)  3.84 us
  transfers between devices with their start and end apart: 3, of which 1 were waited for; matrix products, arithmetic and copies ran while one was open for 9% of the time, Pallas kernels for 0%

profile of v1, /device:TPU:1, one launch (start us, length us, event | category | flops | bytes accessed | tf_op | source)
XLA Modules:
  0.0 146.0 jit_solution(11486843459742263428)
XLA Ops:
  0.0 0.0 copy-start.1
  0.0 5.6 %collective-permute-start.1 = (bf16[2,64,1024]{2,1,0:T(8,128)(2,1)}, bf16[2,64,1024]{2,1,0:T(8,128)(2,1)S(1)}, u32[]{:S(2)}, u32[]{:S(2)}) collective-permute-start(bf16[2,64,1024]{2,1,0:T(8,128)(2,1)} %param.3), channel_id=1, source_target_pairs={{0,3},{1,0},{2,1},{3,2},{4,7},{5,4},{6,5},{7,6},{8,11},{9,8},{10,9... | collective-permute-start | bytes 786440 | tf_op jit(solution)/shard_map/ppermute | solution.py:35
  5.6 1.9 %collective-permute-start = (bf16[2,64,1024]{2,1,0:T(8,128)(2,1)}, bf16[2,64,1024]{2,1,0:T(8,128)(2,1)S(1)}, u32[]{:S(2)}, u32[]{:S(2)}) collective-permute-start(bf16[2,64,1024]{2,1,0:T(8,128)(2,1)} %param.3), channel_id=1, source_target_pairs={{0,1},{1,2},{2,3},{3,0},{4,5},{5,6},{6,7},{7,4},{8,9},{9,10},{10,1... | collective-permute-start | bytes 786440 | tf_op jit(solution)/shard_map/ppermute | solution.py:30
  7.5 3.9 %copy.6 = bf16[16,512,128]{1,2,0:T(8,128)(2,1)} copy(bf16[16,512,128]{2,1,0:T(8,128)(2,1)} %param.4) | data formatting | bytes 4194304 | tf_op args[1]
  11.5 1.7 %slice_negate_fusion.1 = (bf16[16,512,64]{1,2,0:T(8,128)(2,1)S(1)}, bf16[16,512,64]{1,2,0:T(8,128)(2,1)S(1)}) fusion(bf16[16,512,128]{1,2,0:T(8,128)(2,1)} %copy.6), kind=kLoop, calls=%fused_computation.5 | loop fusion | flops 524288 | bytes 4194304 | tf_op jit(solution)/shard_map/neg | solution.py:12
  13.1 0.0 copy-done.1
  13.2 0.0 copy-start.2
  13.2 0.9 slice_negate_fusion
  14.0 0.7 copy-done.2
  14.7 2.2 %maximum_maximum_fusion = bf16[16,1024,128]{1,2,0:T(8,128)(2,1)} fusion(bf16[16,512,64]{1,2,0:T(8,128)(2,1)S(1)} %get-tuple-element.8, bf16[16,512,64]{1,2,0:T(8,128)(2,1)S(1)} %get-tuple-element.7, bf16[16,512,128]{1,2,0:T(8,128)(2,1)S(1)} %copy-done.2), kind=kLoop, calls=%fused_computation | loop fusion | flops 12582912 | bytes 8388608 | tf_op jit(solution)/shard_map/concatenate | solution.py:13
  17.0 0.0 copy-start.3
  17.0 3.6 %maximum_maximum_fusion.1 = bf16[8,16,128,128]{3,2,1,0:T(8,128)(2,1)} fusion(bf16[8,16,64,64]{3,2,1,0:T(8,128)(2,1)S(1)} %get-tuple-element.6, bf16[8,16,64,64]{3,2,1,0:T(8,128)(2,1)S(1)} %get-tuple-element.5, bf16[8,16,64,128]{3,2,1,0:T(8,128)(2,1)S(1)} %copy-done.1), kind=kLoop, calls=%fused_computation.1 | loop fusion | flops 12582912 | bytes 8388608 | tf_op jit(solution)/shard_map/concatenate | solution.py:13
  20.5 0.0 collective-permute-done
  20.5 1.9 %collective-permute-start.2 = (bf16[2,64,1024]{2,1,0:T(8,128)(2,1)S(1)}, bf16[2,64,1024]{2,1,0:T(8,128)(2,1)S(1)}, u32[]{:S(2)}, u32[]{:S(2)}) collective-permute-start(bf16[2,64,1024]{2,1,0:T(8,128)(2,1)S(1)} %collective-permute-done), channel_id=1, source_target_pairs={{0,1},{1,2},{2,3},{3,0},{4,5},{5,6},{6,7},{7,4},{8,9},{9,10},{10,1... | collective-permute-start | bytes 786440 | tf_op jit(solution)/shard_map/ppermute | solution.py:30
  22.4 0.1 broadcast_in_dim.3
  22.6 0.0 copy-done.3
  22.7 0.0 collective-permute-done.1
  22.7 6.1 %collective-permute-done.2 = bf16[2,64,1024]{2,1,0:T(8,128)(2,1)S(1)} collective-permute-done((bf16[2,64,1024]{2,1,0:T(8,128)(2,1)S(1)}, bf16[2,64,1024]{2,1,0:T(8,128)(2,1)S(1)}, u32[]{:S(2)}, u32[]{:S(2)}) %collective-permute-start.2) | collective-permute-done | bytes 262176 | tf_op jit(solution)/shard_map/ppermute | solution.py:30
  28.9 0.0 copy-start
  28.9 4.7 %convolution_convert_fusion = bf16[512,2048]{1,0:T(8,128)(2,1)S(1)} fusion(bf16[512,1024]{1,0:T(8,128)(2,1)S(1)} %bitcast.17, bf16[1024,2048]{0,1:T(8,128)(2,1)} %bitcast.16), kind=kOutput, calls=%fused_computation.2 | convolution fusion | flops 2148532224 | bytes 7340032 | tf_op jit(solution)/shard_map/dot_general | solution.py:41
  33.6 0.0 copy-done
  33.6 0.9 convolution_bitcast_fusion
  34.5 111.0 %psum.7 = f32[8192]{0:T(1024)S(1)} all-reduce(f32[8192]{0:T(1024)S(1)} %convolution_bitcast_fusion), channel_id=1, replica_groups=mesh['cuts'=128,'stem'=4] {'cuts','stem'}, use_global_device_ids=true, to_apply=%region_0.1 | all-reduce | flops 8192 | bytes 65536 | tf_op jit(solution)/shard_map/psum | solution.py:47
  145.4 0.6 dynamic_slice.3
  (4 shorter events, 0.1 us)
Async XLA Ops:
  0.0 13.1 %copy-start.1 = (bf16[8,16,64,128]{3,2,1,0:T(8,128)(2,1)S(1)}, bf16[8,16,64,128]{3,2,1,0:T(8,128)(2,1)}, u32[]{:S(2)}) copy-start(bf16[8,16,64,128]{3,2,1,0:T(8,128)(2,1)} %param.5) | copy-start | bytes 6291460
  0.0 22.7 %collective-permute-start.1 = (bf16[2,64,1024]{2,1,0:T(8,128)(2,1)}, bf16[2,64,1024]{2,1,0:T(8,128)(2,1)S(1)}, u32[]{:S(2)}, u32[]{:S(2)}) collective-permute-start(bf16[2,64,1024]{2,1,0:T(8,128)(2,1)} %param.3), channel_id=1, source_target_pairs={{0,3},{1,0},{2,1},{3,2},{4,7},{5,4},{6,5},{7,6},{8,11},{9,8},{10,9... | collective-permute-start | bytes 786440 | tf_op jit(solution)/shard_map/ppermute | solution.py:35
  5.6 14.9 %collective-permute-start = (bf16[2,64,1024]{2,1,0:T(8,128)(2,1)}, bf16[2,64,1024]{2,1,0:T(8,128)(2,1)S(1)}, u32[]{:S(2)}, u32[]{:S(2)}) collective-permute-start(bf16[2,64,1024]{2,1,0:T(8,128)(2,1)} %param.3), channel_id=1, source_target_pairs={{0,1},{1,2},{2,3},{3,0},{4,5},{5,6},{6,7},{7,4},{8,9},{9,10},{10,1... | collective-permute-start | bytes 786440 | tf_op jit(solution)/shard_map/ppermute | solution.py:30
  13.2 1.6 %copy-start.2 = (bf16[16,512,128]{1,2,0:T(8,128)(2,1)S(1)}, bf16[16,512,128]{1,2,0:T(8,128)(2,1)}, u32[]{:S(2)}) copy-start(bf16[16,512,128]{1,2,0:T(8,128)(2,1)} %copy.6) | copy-start | bytes 6291460
  17.0 5.6 %copy-start.3 = (bf16[2,64,1024]{2,1,0:T(8,128)(2,1)S(1)}, bf16[2,64,1024]{2,1,0:T(8,128)(2,1)}, u32[]{:S(2)}) copy-start(bf16[2,64,1024]{2,1,0:T(8,128)(2,1)} %param.3) | copy-start | bytes 786436
  20.5 8.3 %collective-permute-start.2 = (bf16[2,64,1024]{2,1,0:T(8,128)(2,1)S(1)}, bf16[2,64,1024]{2,1,0:T(8,128)(2,1)S(1)}, u32[]{:S(2)}, u32[]{:S(2)}) collective-permute-start(bf16[2,64,1024]{2,1,0:T(8,128)(2,1)S(1)} %collective-permute-done), channel_id=1, source_target_pairs={{0,1},{1,2},{2,3},{3,0},{4,5},{5,6},{6,7},{7,4},{8,9},{9,10},{10,1... | collective-permute-start | bytes 786440 | tf_op jit(solution)/shard_map/ppermute | solution.py:30
  28.9 4.7 %copy-start = (bf16[8,16,128,128]{3,2,1,0:T(8,128)(2,1)S(1)}, bf16[8,16,128,128]{3,2,1,0:T(8,128)(2,1)}, u32[]{:S(2)}) copy-start(bf16[8,16,128,128]{3,2,1,0:T(8,128)(2,1)} %maximum_maximum_fusion.1) | copy-start | bytes 12582916
